TPU v7x, 32 devices: a whole 2x2x4 slice. The times are simulated.
32 devices in a mesh: dp: 8 (over y, x, core), tp: 4 (over z).
Axes of the slice: x: 2, y: 2, z: 4, core: 2. Of those that a mesh axis runs over, the one named last changes fastest.
Arguments:
- inputs: bfloat16 [26624, 768], P(('dp', 'tp')), may hold values from -6 to 6
- segment_ids: int32 [32, 832], P('dp'), may hold values from -1 to 4, as said below
- mask_flags: int32 [32, 832], P(('dp', 'tp')), may hold values 0 or 1
- mask_token: bfloat16 [768], replicated, may hold values from -6 to 6
- norm_gain: bfloat16 [768], replicated, may hold values from 0.5 to 1.5
- norm_shift: bfloat16 [768], replicated, may hold values from -3 to 3
- heads_weight: bfloat16 [768, 12, 192], P(None, 'tp'), may hold values from -0.21875 to 0.21875
- heads_bias: bfloat16 [12, 128], P('tp'), may hold values from -1.1953125 to 1.1953125
- proj_weight: bfloat16 [768, 768], P('tp'), may hold values from -1.75 to 1.75
- proj_bias: bfloat16 [768], replicated, may hold values from -2 to 2
- attn_scale: bfloat16 [768], replicated, may hold values from 0.5 to 1.5
- mlp_gain: bfloat16 [768], replicated, may hold values from 0.5 to 1.5
- mlp_shift: bfloat16 [768], replicated, may hold values from -3 to 3
- up_weight: bfloat16 [768, 3072], P(None, 'tp'), may hold values from -0.21875 to 0.21875
- up_bias: bfloat16 [3072], P('tp'), may hold values from -2 to 2
- down_weight: bfloat16 [3072, 768], P('tp'), may hold values from -0.109375 to 0.109375
- down_bias: bfloat16 [768], replicated, may hold values from -2 to 2
- mlp_scale: bfloat16 [768], replicated, may hold values from 0.5 to 1.5
- grad_out: bfloat16 [26624, 768], P(('dp', 'tp')), may hold values from -6 to 6
Outputs:
- output: bfloat16 [26624, 768], P(('dp', 'tp'))
- grad_inputs: float32 [26624, 768], P(('dp', 'tp'))
- grad_token: float32 [768], replicated
- grad_norm_gain: float32 [768], replicated
- grad_norm_shift: float32 [768], replicated
- grad_heads_weight: float32 [768, 12, 192], P(None, 'tp')
- grad_heads_bias: float32 [12, 128], P('tp')
- grad_proj_weight: float32 [768, 768], P('tp')
- grad_proj_bias: float32 [768], replicated
- grad_attn_scale: float32 [768], replicated
- grad_mlp_gain: float32 [768], replicated
- grad_mlp_shift: float32 [768], replicated
- grad_up_weight: float32 [768, 3072], P(None, 'tp')
- grad_up_bias: float32 [3072], P('tp')
- grad_down_weight: float32 [3072, 768], P('tp')
- grad_down_bias: float32 [768], replicated
- grad_mlp_scale: float32 [768], replicated
Inputs may be any that keep to these rules, and one draw needn't show every extreme that they name: `segment_ids`: every packed row holds five images numbered 0 to 4 in order from its first slot, then 1 to 32 padding slots marked -1 at its end; each of the first four images has h * w + 1 slots with h and w from 11 to 14, the fifth fills the rest.
All inputs are finite; a program needn't handle non-finite values. No bound on the sum of `mask_flags` on one device may be relied on, other than what follows from the above.
Results may differ from a plain program's by a relative error of at most 0.02.
Values may be sent and summed in bfloat16 or wider, within the bound.
A program may use at most 192 MiB of HBM per device.

v0:
```python
import jax
import jax.numpy as jnp
from jax import lax
from jax.sharding import PartitionSpec as P

EPSILON = 1e-06
FLOOR_SCORE = -1e30
SQRT_HALF = 0.7071067811865476
INV_ROOT_TWO_PI = 0.3989422804014327


def layer_norm(values, gain, shift):
    centre = values - jnp.mean(values, axis=-1, keepdims=True)
    inverse = lax.rsqrt(jnp.mean(centre * centre, axis=-1, keepdims=True) + EPSILON)
    scaled = centre * inverse
    return (scaled * gain + shift, scaled, inverse)


def norm_back(grad_normed, scaled, inverse, gain):
    grad_scaled = grad_normed * gain
    first = jnp.mean(grad_scaled, axis=-1, keepdims=True)
    second = jnp.mean(grad_scaled * scaled, axis=-1, keepdims=True)
    return inverse * (grad_scaled - first - scaled * second)


def gelu_parts(inner):
    normal_cdf = 0.5 * (1.0 + lax.erf(inner * SQRT_HALF))
    density = jnp.exp(-0.5 * inner * inner) * INV_ROOT_TWO_PI
    return (inner * normal_cdf, normal_cdf + inner * density)


def head_bias_row(bias, head_size):
    blank = jnp.zeros((bias.shape[0], head_size), jnp.float32)
    joined = jnp.concatenate(
        [bias[:, :head_size].astype(jnp.float32), blank, bias[:, head_size:].astype(jnp.float32)],
        axis=1,
    )
    return joined.reshape(-1)


def split_block(block, head_size):
    return (
        block[..., :head_size],
        block[..., head_size : 2 * head_size],
        block[..., 2 * head_size :],
    )


def row_scores(query, keys, groups, scale):
    scores = jnp.einsum("qhd,khd->hqk", query, keys, preferred_element_type=jnp.float32) * scale
    same = groups[:, None] == groups[None, :]
    return jnp.where(same[None], scores, FLOOR_SCORE)


def forward_row(block, groups, head_size, scale):
    query, keys, values = split_block(block, head_size)
    scores = row_scores(query, keys, groups, scale)
    largest = jnp.max(scores, axis=-1, keepdims=True)
    raised = jnp.exp(scores - largest)
    total = jnp.sum(raised, axis=-1, keepdims=True)
    shares = (raised / total).astype(jnp.bfloat16)
    mixed = jnp.einsum("hqk,khd->qhd", shares, values, preferred_element_type=jnp.float32).astype(
        jnp.bfloat16
    )
    return (mixed, largest + jnp.log(total))


def backward_row(block, groups, log_total, grad_mixed, head_size, scale):
    query, keys, values = split_block(block, head_size)
    scores = row_scores(query, keys, groups, scale)
    shares = jnp.exp(scores - log_total)
    grad_shares = jnp.einsum("qhd,khd->hqk", grad_mixed, values, preferred_element_type=jnp.float32)
    centre = jnp.sum(shares * grad_shares, axis=-1, keepdims=True)
    grad_scores = (shares * (grad_shares - centre)).astype(jnp.bfloat16)
    grad_query = (
        jnp.einsum("hqk,khd->qhd", grad_scores, keys, preferred_element_type=jnp.float32) * scale
    )
    grad_keys = (
        jnp.einsum("hqk,qhd->khd", grad_scores, query, preferred_element_type=jnp.float32) * scale
    )
    grad_values = jnp.einsum(
        "hqk,qhd->khd", shares.astype(jnp.bfloat16), grad_mixed, preferred_element_type=jnp.float32
    )
    return jnp.concatenate([grad_query, grad_keys, grad_values], axis=-1).astype(jnp.bfloat16)


def local(
    inputs,
    segment_ids,
    mask_flags,
    mask_token,
    norm_gain,
    norm_shift,
    heads_weight,
    heads_bias,
    proj_weight,
    proj_bias,
    attn_scale,
    mlp_gain,
    mlp_shift,
    up_weight,
    up_bias,
    down_weight,
    down_bias,
    mlp_scale,
    grad_out,
):
    own_rows, slots = mask_flags.shape
    width = inputs.shape[1]
    triple = heads_weight.shape[2]
    head_size = triple // 3
    scale = head_size ** (-0.5)
    own_ids = lax.dynamic_slice_in_dim(segment_ids, lax.axis_index("tp") * own_rows, own_rows, 0)
    valid = (own_ids.reshape(-1, 1) >= 0).astype(jnp.float32)
    flagged = (mask_flags.reshape(-1, 1) == 1).astype(jnp.float32)
    start_x = valid * (
        flagged * mask_token.astype(jnp.float32) + (1.0 - flagged) * inputs.astype(jnp.float32)
    )
    first_gain = norm_gain.astype(jnp.float32)
    second_gain = mlp_gain.astype(jnp.float32)
    normed1, scaled1, inverse1 = layer_norm(start_x, first_gain, norm_shift.astype(jnp.float32))
    normed1 = normed1.astype(jnp.bfloat16)
    all_heads, all_heads_bias, all_proj, all_up, all_up_bias, all_down = (
        heads_weight,
        heads_bias,
        proj_weight,
        up_weight,
        up_bias,
        down_weight,
    )
    heads_now = all_heads.shape[1]
    flat_heads = all_heads.reshape(width, heads_now * triple)
    bias_row = head_bias_row(all_heads_bias, head_size)
    up_bias_float = all_up_bias.astype(jnp.float32)
    rows_count = segment_ids.shape[0]

    def project(piece):
        return (jnp.dot(piece, flat_heads, preferred_element_type=jnp.float32) + bias_row).astype(
            jnp.bfloat16
        )

    packed = project(lax.all_gather(normed1, "tp", axis=0, tiled=True))
    blocks = packed.reshape(rows_count, slots, heads_now, triple)
    mixed, log_total = lax.map(
        lambda item: forward_row(item[0], item[1], head_size, scale), (blocks, segment_ids)
    )
    mixed = mixed.reshape(-1, heads_now * head_size)
    rows = mixed
    attended = lax.psum_scatter(
        jnp.dot(rows, all_proj, preferred_element_type=jnp.float32).astype(jnp.bfloat16),
        "tp",
        scatter_dimension=0,
        tiled=True,
    ).astype(jnp.float32)
    branch1 = attended + proj_bias.astype(jnp.float32)
    middle = start_x + attn_scale.astype(jnp.float32) * branch1
    normed2, scaled2, inverse2 = layer_norm(middle, second_gain, mlp_shift.astype(jnp.float32))
    normed2 = normed2.astype(jnp.bfloat16)
    unit_value, derivative = gelu_parts(
        jnp.dot(
            lax.all_gather(normed2, "tp", axis=0, tiled=True),
            all_up,
            preferred_element_type=jnp.float32,
        )
        + up_bias_float
    )
    hidden = unit_value.astype(jnp.bfloat16)
    rows = hidden
    summed = lax.psum_scatter(
        jnp.dot(rows, all_down, preferred_element_type=jnp.float32).astype(jnp.bfloat16),
        "tp",
        scatter_dimension=0,
        tiled=True,
    ).astype(jnp.float32)
    branch2 = summed + down_bias.astype(jnp.float32)
    output = (valid * (middle + mlp_scale.astype(jnp.float32) * branch2)).astype(jnp.bfloat16)
    grad_final = valid * grad_out.astype(jnp.float32)
    grad_scale2 = jnp.sum(branch2 * grad_final, axis=0)
    grad_branch2 = mlp_scale.astype(jnp.float32) * grad_final
    grad_down_bias = jnp.sum(grad_branch2, axis=0)
    grad_low2 = grad_branch2.astype(jnp.bfloat16)
    rows_norm2, rows_grad2 = (
        lax.all_gather(normed2, "tp", axis=0, tiled=True),
        lax.all_gather(grad_low2, "tp", axis=0, tiled=True),
    )
    unit_input = jnp.dot(rows_norm2, all_up, preferred_element_type=jnp.float32) + up_bias_float
    unit_value, derivative = gelu_parts(unit_input)
    unit_low = unit_value.astype(jnp.bfloat16)
    grad_unit = (
        jnp.dot(rows_grad2, all_down.T, preferred_element_type=jnp.float32) * derivative
    ).astype(jnp.bfloat16)
    grad_up = jnp.dot(rows_norm2.T, grad_unit, preferred_element_type=jnp.float32)
    grad_up_bias = jnp.sum(grad_unit, axis=0, dtype=jnp.float32)
    grad_down = jnp.dot(unit_low.T, rows_grad2, preferred_element_type=jnp.float32)
    rows = grad_unit
    grad_normed2 = lax.psum_scatter(
        jnp.dot(rows, all_up.T, preferred_element_type=jnp.float32).astype(jnp.bfloat16),
        "tp",
        scatter_dimension=0,
        tiled=True,
    ).astype(jnp.float32)
    grad_gain2 = jnp.sum(grad_normed2 * scaled2, axis=0)
    grad_shift2 = jnp.sum(grad_normed2, axis=0)
    grad_middle = grad_final + norm_back(grad_normed2, scaled2, inverse2, second_gain)
    grad_scale1 = jnp.sum(branch1 * grad_middle, axis=0)
    grad_branch1 = attn_scale.astype(jnp.float32) * grad_middle
    grad_proj_bias = jnp.sum(grad_branch1, axis=0)
    grad_low1 = grad_branch1.astype(jnp.bfloat16)
    rows_norm1, rows_grad1 = (
        lax.all_gather(normed1, "tp", axis=0, tiled=True),
        lax.all_gather(grad_low1, "tp", axis=0, tiled=True),
    )
    packed_again = project(rows_norm1).reshape(rows_count, slots, heads_now, triple)
    grad_proj = jnp.dot(mixed.T, rows_grad1, preferred_element_type=jnp.float32)
    grad_mixed = jnp.dot(rows_grad1, all_proj.T, preferred_element_type=jnp.float32).astype(
        jnp.bfloat16
    )
    grad_mixed = grad_mixed.reshape(rows_count, slots, heads_now, head_size)
    grad_blocks = lax.map(
        lambda item: backward_row(item[0], item[1], item[2], item[3], head_size, scale),
        (packed_again, segment_ids, log_total, grad_mixed),
    )
    grad_packed = grad_blocks.reshape(-1, heads_now * triple)
    grad_heads = jnp.dot(rows_norm1.T, grad_packed, preferred_element_type=jnp.float32).reshape(
        width, heads_now, triple
    )
    bias_sums = jnp.sum(grad_packed, axis=0, dtype=jnp.float32).reshape(heads_now, triple)
    grad_heads_bias = jnp.concatenate(
        [bias_sums[:, :head_size], bias_sums[:, 2 * head_size :]], axis=1
    )
    rows = grad_packed
    grad_normed1 = lax.psum_scatter(
        jnp.dot(rows, flat_heads.T, preferred_element_type=jnp.float32).astype(jnp.bfloat16),
        "tp",
        scatter_dimension=0,
        tiled=True,
    ).astype(jnp.float32)
    grad_gain1 = jnp.sum(grad_normed1 * scaled1, axis=0)
    grad_shift1 = jnp.sum(grad_normed1, axis=0)
    grad_start = grad_middle + norm_back(grad_normed1, scaled1, inverse1, first_gain)
    grad_inputs = valid * (1.0 - flagged) * grad_start
    grad_token = jnp.sum(valid * flagged * grad_start, axis=0)
    local_grads = (grad_heads, grad_heads_bias, grad_proj, grad_up, grad_up_bias, grad_down)
    sum_heads, sum_heads_bias, sum_proj, sum_up, sum_up_bias, sum_down = lax.psum(
        (
            local_grads[0],
            local_grads[1],
            local_grads[2],
            local_grads[3],
            local_grads[4],
            local_grads[5],
        ),
        "dp",
    )
    (
        sum_token,
        sum_gain1,
        sum_shift1,
        sum_proj_bias,
        sum_scale1,
        sum_gain2,
        sum_shift2,
        sum_down_bias,
        sum_scale2,
    ) = lax.psum(
        (
            grad_token,
            grad_gain1,
            grad_shift1,
            grad_proj_bias,
            grad_scale1,
            grad_gain2,
            grad_shift2,
            grad_down_bias,
            grad_scale2,
        ),
        ("dp", "tp"),
    )
    return (
        output,
        grad_inputs,
        sum_token,
        sum_gain1,
        sum_shift1,
        sum_heads,
        sum_heads_bias,
        sum_proj,
        sum_proj_bias,
        sum_scale1,
        sum_gain2,
        sum_shift2,
        sum_up,
        sum_up_bias,
        sum_down,
        sum_down_bias,
        sum_scale2,
    )


def solution(mesh):
    placed = (
        P(("dp", "tp"), None),
        P("dp", None),
        P(("dp", "tp"), None),
        P(),
        P(),
        P(),
        P(None, "tp", None),
        P("tp", None),
        P("tp", None),
        P(),
        P(),
        P(),
        P(),
        P(None, "tp"),
        P("tp"),
        P("tp", None),
        P(),
        P(),
        P(("dp", "tp"), None),
    )
    return jax.shard_map(
        local,
        mesh=mesh,
        in_specs=placed,
        out_specs=(
            P(("dp", "tp"), None),
            P(("dp", "tp"), None),
            P(),
            P(),
            P(),
            P(None, "tp", None),
            P("tp", None),
            P("tp", None),
            P(),
            P(),
            P(),
            P(),
            P(None, "tp"),
            P("tp"),
            P("tp", None),
            P(),
            P(),
        ),
        check_vma=False,
    )
```

profile of v0, /device:TPU:0, one launch (start us, length us, event | category | flops | bytes accessed | tf_op | source)
XLA Modules:
  0.0 1097.8 jit_solution(15875236159607952465)
XLA Ops:
  10.9 2.1 fusion.69
  13.0 2.2 multiply_reduce_fusion.5
  17.5 98.4 %all-gather.5.cloned.1.call-done = bf16[3328,768]{1,0:T(8,128)(2,1)} async-done(((bf16[832,768]{1,0:T(8,128)(2,1)}), bf16[3328,768]{1,0:T(8,128)(2,1)}) %all-gather.5.cloned.1.call-update) | async-done | bytes 5111824 | tf_op jit(solution)/shard_map/all_gather | solution.py:142
  115.9 7.7 add_convert_fusion
  123.6 9.7 reshape.283
  133.3 4.8 copy.47
  138.1 37.2 %while.22 = (s32[]{:T(128)}, bf16[4,832,3,64]{1,3,2,0:T(8,128)(2,1)}, f32[4,3,832,1]{2,1,3,0:T(4,128)S(1)}, bf16[4,832,3,192]{1,3,2,0:T(8,128)(2,1)}, s32[4,832]{1,0:T(4,128)S(1)}, /*index=5*/s32[]{:T(128)}) while((s32[]{:T(128)}, bf16[4,832,3,64]{1,3,2,0:T(8,128)(2,1)}, f32[4,3,832,1]{2,1,3,0:T(4,128)S(1)}, ...), condition=%wide.region_5.6_spmd, body=%wide.region_2.5_spmd.sunk | while | flops 557397568 | bytes 31839324 | solution.py:144
  139.9 1.9 fusion.120
  141.8 2.0 fusion.121
  143.8 3.5 fusion.122
  151.1 2.0 fusion.121
  153.1 3.5 fusion.122
  158.5 1.9 fusion.120
  160.4 2.0 fusion.121
  162.4 3.5 fusion.122
  169.8 2.0 fusion.121
  171.8 3.5 fusion.122
  175.3 3.5 copy.48
  178.9 4.1 reshape.284
  183.0 5.1 convolution_convert_fusion.1
  188.9 89.5 %reduce-scatter.5.cloned.1.call-done = bf16[832,768]{1,0:T(8,128)(2,1)} async-done(((bf16[3328,768]{1,0:T(8,128)(2,1)}), bf16[832,768]{1,0:T(8,128)(2,1)}) %reduce-scatter.5.cloned.1.call-update) | async-done | bytes 1277968 | tf_op jit(solution)/shard_map/reduce_scatter | solution.py:149
  278.4 3.7 fusion.73
  285.8 95.9 %all-gather.7.cloned.1.call-done = bf16[3328,768]{1,0:T(8,128)(2,1)} async-done(((bf16[832,768]{1,0:T(8,128)(2,1)}), bf16[3328,768]{1,0:T(8,128)(2,1)}) %all-gather.7.cloned.1.call-update) | async-done | bytes 5111824 | tf_op jit(solution)/shard_map/all_gather | solution.py:161
  381.7 10.1 multiply_convert_fusion.1
  391.7 86.3 %all-gather.9.cloned.1.call-done = bf16[3328,768]{1,0:T(8,128)(2,1)} async-done(((bf16[832,768]{1,0:T(8,128)(2,1)}), bf16[3328,768]{1,0:T(8,128)(2,1)}) %all-gather.9.cloned.1.call-update) | async-done | bytes 5111824 | tf_op jit(solution)/shard_map/all_gather | solution.py:184
  478.0 10.3 convert_reduce_fusion
  488.3 2.3 copy-done.52
  490.6 5.9 convolution_convert_fusion.2
  496.6 8.3 convolution_convert_fusion.3
  505.6 81.1 %reduce-scatter.9.cloned.1.call-done = bf16[832,768]{1,0:T(8,128)(2,1)} async-done(((bf16[3328,768]{1,0:T(8,128)(2,1)}), bf16[832,768]{1,0:T(8,128)(2,1)}) %reduce-scatter.9.cloned.1.call-update) | async-done | bytes 1277968 | tf_op jit(solution)/shard_map/reduce_scatter | solution.py:196
  586.7 3.1 fusion.63
  589.8 91.3 %reduce-scatter.7.cloned.1.call-done = bf16[832,768]{1,0:T(8,128)(2,1)} async-done(((bf16[3328,768]{1,0:T(8,128)(2,1)}), bf16[832,768]{1,0:T(8,128)(2,1)}) %reduce-scatter.7.cloned.1.call-update) | async-done | bytes 1277968 | tf_op jit(solution)/shard_map/reduce_scatter | solution.py:169
  681.1 5.3 multiply_reduce_fusion.2
  689.2 96.5 %all-gather.11.cloned.1.call-done = bf16[3328,768]{1,0:T(8,128)(2,1)} async-done(((bf16[832,768]{1,0:T(8,128)(2,1)}), bf16[3328,768]{1,0:T(8,128)(2,1)}) %all-gather.11.cloned.1.call-update) | async-done | bytes 5111824 | tf_op jit(solution)/shard_map/all_gather | solution.py:211
  785.7 4.3 convolution_convert_fusion.4
  792.0 57.7 %while.23 = (s32[]{:T(128)}, bf16[4,832,3,192]{1,3,2,0:T(8,128)(2,1)}, bf16[4,832,3,192]{1,3,2,0:T(8,128)(2,1)}, s32[4,832]{1,0:T(4,128)S(1)}, f32[4,3,832,1]{2,...) while((s32[]{:T(128)}, bf16[4,832,3,192]{1,3,2,0:T(8,128)(2,1)}, ...), condition=%wide.region_15.16_spmd, body=%wide.region_13.15_spmd.sunk | while | flops 1364583936 | bytes 74455664 | solution.py:219
  795.3 2.5 fusion.132
  797.7 2.9 multiply_reduce_fusion.8
  800.6 2.5 multiply_convert_fusion.5
  809.7 2.5 fusion.132
  812.1 2.9 multiply_reduce_fusion.8
  815.0 2.5 multiply_convert_fusion.5
  824.1 2.5 fusion.132
  826.5 2.9 multiply_reduce_fusion.8
  829.4 2.5 multiply_convert_fusion.5
  838.4 2.5 fusion.132
  840.9 2.9 multiply_reduce_fusion.8
  843.8 2.5 multiply_convert_fusion.5
  849.8 7.3 copy.51
  857.1 8.1 reshape.286
  865.2 8.1 convolution_convert_fusion
  873.4 9.8 fusion.77
  883.2 9.8 fusion.76
  893.0 2.0 fusion.75
  895.0 4.5 fusion.47
  899.7 3.2 convert_reduce_fusion.1
  903.0 14.6 %all-reduce.1 = (f32[3,128]{1,0:T(4,128)}, f32[768]{0:T(1024)}) all-reduce(f32[3,128]{1,0:T(4,128)S(1)} %pad_maximum_fusion.1, f32[768]{0:T(1024)S(1)} %copy-done.42), channel_id=1, replica_groups=mesh['dp'=8,'tp'=4] {'dp'}, use_global_device_ids=true, to_apply=%region_27.28 | all-reduce | flops 1152 | bytes 9216 | tf_op jit(solution)/shard_map/psum | solution.py:244
  917.6 45.9 %reduce-scatter.11.cloned.1.call-done = bf16[832,768]{1,0:T(8,128)(2,1)} async-done(((bf16[3328,768]{1,0:T(8,128)(2,1)}), bf16[832,768]{1,0:T(8,128)(2,1)}) %reduce-scatter.11.cloned.1.call-update) | async-done | bytes 1277968 | tf_op jit(solution)/shard_map/reduce_scatter | solution.py:232
  963.6 4.2 fusion.64
  968.0 2.9 multiply_reduce_fusion.3
  970.9 42.5 %all-reduce = (f32[768]{0:T(1024)}, f32[768]{0:T(1024)}, f32[768]{0:T(1024)}, f32[768]{0:T(1024)}, f32[768]{0:T(1024)}, /*index=5*/f32[768]{0:T(1024)}, f32[768]{0:T(1024)}, f32[768]{0:T(1024)}, f32[768]{0:T(1024)}) all-reduce(f32[768]{0:T(1024)S(1)} %get-tuple-element.154, ...), channel_id=1, replica_groups=mesh['dp'=8,'tp'=4] {'dp','tp'}, use_global_device_ids=true, to_apply=%region_20.21 | all-reduce | flops 6912 | bytes 55296 | tf_op jit(solution)/shard_map/psum | solution.py:265
  1013.4 3.4 broadcast_multiply_fusion
  1016.8 66.3 %all-reduce.5.cloned.1.call-done = (f32[768,3,192]{0,2,1:T(8,128)}, f32[192,768]{1,0:T(8,128)}, f32[768,768]{1,0:T(8,128)}, f32[768,768]{1,0:T(8,128)}) async-done(((f32[768,3,192]{0,2,1:T(8,128)}, f32[192,768]{1,0:T(8,128)}, f32[768,768]{1,0:T(8,128)}, f32[768,768]{1,0:T(8,128)}), (f32[768,3,192]{0,2,1:T(8,128)}, f32[192,768]{1,0:T(8,128)}, f32[768,768]{1,0:T(8,128)}, ...) | async-done | bytes 7077904 | tf_op jit(solution)/shard_map/psum | solution.py:244
  1083.1 2.9 copy.80
  (224 shorter events, 58.0 us)
Async XLA Ops:
  7.2 374.5 %copy-start = (bf16[768,768]{1,0:T(8,128)(2,1)S(1)}, bf16[768,768]{1,0:T(8,128)(2,1)}, u32[]{:S(2)}) copy-start(bf16[768,768]{1,0:T(8,128)(2,1)} %param.36) | copy-start | bytes 3538948
  7.2 8.1 copy-start.4
  7.2 108.7 %all-gather.5.cloned.1.call-start = ((), (), s32[]{:S(2)}) async-start(), calls=%async_computation.4 | async-start | bytes 6389760 | tf_op jit(solution)/shard_map/all_gather | solution.py:142
  8.2 672.9 %copy-start.16 = (f32[832]{0:T(1024)}, f32[832]{0:T(1024)S(1)}, u32[]{:S(2)}) copy-start(f32[832]{0:T(1024)S(1)} %convert_element_type.152) | copy-start | bytes 9988
  8.2 270.2 %copy-start.18 = (f32[832]{0:T(1024)}, f32[832]{0:T(1024)S(1)}, u32[]{:S(2)}) copy-start(f32[832]{0:T(1024)S(1)} %convert_element_type.153) | copy-start | bytes 9988
  8.8 269.6 %copy-start.20 = (f32[832]{0:T(1024)}, f32[832]{0:T(1024)S(1)}, u32[]{:S(2)}) copy-start(f32[832]{0:T(1024)S(1)} %get-tuple-element.168) | copy-start | bytes 9988
  9.5 268.9 %copy-start.22 = (f32[768]{0:T(1024)}, f32[768]{0:T(1024)S(1)}, u32[]{:S(2)}) copy-start(f32[768]{0:T(1024)S(1)} %convert_element_type.154) | copy-start | bytes 9220
  10.2 6.9 copy-start.27
  13.0 4.2 copy-start.25
  13.0 4.3 copy-start.41
  15.3 108.3 %copy-start.29 = (f32[832]{0:T(1024)}, f32[832]{0:T(1024)S(1)}, u32[]{:S(2)}) copy-start(f32[832]{0:T(1024)S(1)} %add_rsqrt_fusion.1) | copy-start | bytes 9988
  17.2 261.2 %reduce-scatter.5.cloned.1.call-start = ((), (), s32[]{:S(2)}) async-start(), calls=%async_computation.5 | async-start | bytes 6389760 | tf_op jit(solution)/shard_map/reduce_scatter | solution.py:149
  133.3 4.8 copy-start.24
  175.3 7.7 copy-start.15
  188.2 0.7 copy-start.44
  188.2 0.7 copy-start.45
  188.2 0.7 copy-start.46
  188.2 0.7 copy-start.47
  188.2 193.5 %all-gather.7.cloned.1.call-start = ((), (), s32[]{:S(2)}) async-start(), calls=%async_computation.6 | async-start | bytes 6389760 | tf_op jit(solution)/shard_map/all_gather | solution.py:161
  188.9 492.2 %copy-start.31 = (f32[768]{0:T(1024)}, f32[768]{0:T(1024)S(1)}, u32[]{:S(2)}) copy-start(f32[768]{0:T(1024)S(1)} %convert_element_type.166) | copy-start | bytes 9220
  282.1 1.5 copy-start.2
  283.6 2.2 copy-start.48
  285.1 192.9 %all-gather.9.cloned.1.call-start = ((), (), s32[]{:S(2)}) async-start(), calls=%async_computation.8 | async-start | bytes 6389760 | tf_op jit(solution)/shard_map/all_gather | solution.py:184
  285.7 301.0 %reduce-scatter.9.cloned.1.call-start = ((), (), s32[]{:S(2)}) async-start(), calls=%async_computation.9 | async-start | bytes 6389760 | tf_op jit(solution)/shard_map/reduce_scatter | solution.py:196
  285.8 192.2 %copy-start.50 = (bf16[768,768]{1,0:T(8,128)(2,1)S(1)}, bf16[768,768]{1,0:T(8,128)(2,1)}, u32[]{:S(2)}) copy-start(bf16[768,768]{1,0:T(8,128)(2,1)} %param.38) | copy-start | bytes 3538948
  488.3 2.3 copy-start.52
  496.6 184.5 %reduce-scatter.7.cloned.1.call-start = ((), (), s32[]{:S(2)}) async-start(), calls=%async_computation.7 | async-start | bytes 6389760 | tf_op jit(solution)/shard_map/reduce_scatter | solution.py:169
  504.9 81.8 %copy-start.3 = (f32[832,768]{1,0:T(8,128)S(1)}, f32[832,768]{1,0:T(8,128)}, u32[]{:S(2)}) copy-start(f32[832,768]{1,0:T(8,128)} %copy-done.2) | copy-start | bytes 7667716
  505.0 280.7 %all-gather.11.cloned.1.call-start = ((), (), s32[]{:S(2)}) async-start(), calls=%async_computation.10 | async-start | bytes 6389760 | tf_op jit(solution)/shard_map/all_gather | solution.py:211
  505.6 180.7 %copy-start.33 = (f32[768]{0:T(1024)}, f32[768]{0:T(1024)S(1)}, u32[]{:S(2)}) copy-start(f32[768]{0:T(1024)S(1)} %convert_element_type.174) | copy-start | bytes 9220
  686.4 1.5 copy-start.6
  689.1 274.4 %reduce-scatter.11.cloned.1.call-start = ((), (), s32[]{:S(2)}) async-start(), calls=%async_computation.11 | async-start | bytes 6389760 | tf_op jit(solution)/shard_map/reduce_scatter | solution.py:232
  857.1 8.1 copy-start.51
  873.3 209.8 %all-reduce.5.cloned.1.call-start = ((), (), s32[]{:S(2)}) async-start(), calls=%async_computation.12 | async-start | bytes 14155776 | tf_op jit(solution)/shard_map/psum | solution.py:244
  873.4 19.6 %slice-start.2 = ((s8[5111808]{0:T(1024)(128)(4,1)}), s8[4194304]{0:T(1024)(128)(4,1)S(1)}, s32[]{:S(2)}) async-start(s8[5111808]{0:T(1024)(128)(4,1)} %bitcast.100), calls=%async_computation.15 | async-start | bytes 8388608
  873.4 21.6 %slice-start = ((s8[5111808]{0:T(1024)(128)(4,1)}), s8[4194304]{0:T(1024)(128)(4,1)S(1)}, s32[]{:S(2)}) async-start(s8[5111808]{0:T(1024)(128)(4,1)} %bitcast.98), calls=%async_computation.13 | async-start | bytes 8388608
  883.2 9.8 copy-start.9
  883.2 9.8 slice-start.3
  883.2 11.8 %slice-start.1 = ((s8[5111808]{0:T(1024)(128)(4,1)}), s8[917504]{0:T(1024)(128)(4,1)S(1)}, s32[]{:S(2)}) async-start(s8[5111808]{0:T(1024)(128)(4,1)} %bitcast.98), calls=%async_computation.14 | async-start | bytes 1835008
  892.9 2.1 copy-start.11
  899.5 3.4 copy-start.42
  899.5 64.0 %copy-start.5 = (bf16[832,768]{1,0:T(8,128)(2,1)S(1)}, bf16[832,768]{1,0:T(8,128)(2,1)}, u32[]{:S(2)}) copy-start(bf16[832,768]{1,0:T(8,128)(2,1)} %param.23) | copy-start | bytes 3833860
  899.6 64.0 %copy-start.8 = (bf16[832,768]{1,0:T(8,128)(2,1)S(1)}, bf16[832,768]{1,0:T(8,128)(2,1)}, u32[]{:S(2)}) copy-start(bf16[832,768]{1,0:T(8,128)(2,1)} %param.41) | copy-start | bytes 3833860
  899.6 64.0 %copy-start.17 = (f32[832]{0:T(1024)S(1)}, f32[832]{0:T(1024)}, u32[]{:S(2)}) copy-start(f32[832]{0:T(1024)} %copy-done.16) | copy-start | bytes 9988
  899.6 64.0 %copy-start.19 = (f32[832]{0:T(1024)S(1)}, f32[832]{0:T(1024)}, u32[]{:S(2)}) copy-start(f32[832]{0:T(1024)} %copy-done.18) | copy-start | bytes 9988
  899.6 63.9 %copy-start.21 = (f32[832]{0:T(1024)S(1)}, f32[832]{0:T(1024)}, u32[]{:S(2)}) copy-start(f32[832]{0:T(1024)} %copy-done.20) | copy-start | bytes 9988
  899.6 63.9 %copy-start.23 = (f32[768]{0:T(1024)S(1)}, f32[768]{0:T(1024)}, u32[]{:S(2)}) copy-start(f32[768]{0:T(1024)} %copy-done.22) | copy-start | bytes 9220
  899.6 63.9 %copy-start.26 = (f32[832]{0:T(1024)S(1)}, f32[832]{0:T(1024)}, u32[]{:S(2)}) copy-start(f32[832]{0:T(1024)} %copy-done.25) | copy-start | bytes 9988
  899.6 63.9 %copy-start.28 = (f32[768]{0:T(1024)S(1)}, f32[768]{0:T(1024)}, u32[]{:S(2)}) copy-start(f32[768]{0:T(1024)} %copy-done.27) | copy-start | bytes 9220
  899.6 63.9 %copy-start.30 = (f32[832]{0:T(1024)S(1)}, f32[832]{0:T(1024)}, u32[]{:S(2)}) copy-start(f32[832]{0:T(1024)} %copy-done.29) | copy-start | bytes 9988
  899.6 63.9 %copy-start.32 = (f32[768]{0:T(1024)S(1)}, f32[768]{0:T(1024)}, u32[]{:S(2)}) copy-start(f32[768]{0:T(1024)} %copy-done.31) | copy-start | bytes 9220
  899.7 63.9 %copy-start.34 = (f32[768]{0:T(1024)S(1)}, f32[768]{0:T(1024)}, u32[]{:S(2)}) copy-start(f32[768]{0:T(1024)} %copy-done.33) | copy-start | bytes 9220
  917.6 50.3 %copy-start.35 = (f32[832]{0:T(1024)S(1)}, f32[832]{0:T(1024)}, u32[]{:S(2)}) copy-start(f32[832]{0:T(1024)} %get-tuple-element.167) | copy-start | bytes 9988
  963.6 4.3 copy-start.7
  963.6 4.3 copy-start.10
  967.9 3.0 copy-start.36
  967.9 3.0 copy-start.37
  967.9 3.0 copy-start.38
  967.9 3.0 copy-start.39
  968.0 45.5 %copy-start.40 = (f32[832]{0:T(1024)S(1)}, f32[832]{0:T(1024)}, u32[]{:S(2)}) copy-start(f32[832]{0:T(1024)} %get-tuple-element.166) | copy-start | bytes 9988
  1083.1 3.0 copy-start.14
  1083.1 3.8 copy-start.13
  1086.9 2.5 copy-start.12
  1086.9 3.9 copy-start.1
  (2 other events, 1.4 us)
Sparse Core Ops, SparseCore 0:
  17.3 98.5 all-gather.4
  188.3 90.0 reduce-scatter.4
  285.2 96.3 all-gather.6
  383.7 94.2 all-gather.8
  496.7 89.9 reduce-scatter.8
  588.9 92.1 reduce-scatter.6
  689.2 96.4 all-gather.10
  873.4 90.0 reduce-scatter.10
  968.4 114.7 all-reduce.4
where the time goes:
time: 1100 us
  waiting for transfers between devices  752 us (68%)
  matrix products  143 us (13%)
  other arithmetic  65.3 us (6%)
  local copies, waits for them, and re-layouts  64.4 us (6%)
  blocking collectives  57.1 us (5%)
  between operations  14.9 us (1%)
    all_gather x1, waiting for transfers between devices, local(): packed = project(lax.all_gather(normed1, 'tp', axis=0, tiled=True))  98.4 us
    all_gather x1, waiting for transfers between devices, local(): lax.all_gather(grad_low1, 'tp', axis=0, tiled=True)  96.5 us
    all_gather x1, waiting for transfers between devices, local(): lax.all_gather(normed2, 'tp', axis=0, tiled=True)  95.9 us
    reduce_scatter x1, waiting for transfers between devices, local(): lax.psum_scatter(jnp.dot(rows, all_down, preferred_element_type=jnp.float...  91.3 us
    reduce_scatter x1, waiting for transfers between devices, local(): lax.psum_scatter(jnp.dot(rows, all_proj, preferred_element_type=jnp.float...  89.5 us
    all_gather x1, waiting for transfers between devices, local(): lax.all_gather(grad_low2, 'tp', axis=0, tiled=True)  86.3 us
    reduce_scatter x1, waiting for transfers between devices, local(): lax.psum_scatter(jnp.dot(rows, all_up.T, preferred_element_type=jnp.float...  81.1 us
    psum x1, waiting for transfers between devices, local(): lax.psum((local_grads[0], local_grads[1], local_grads[2], local_grads[3],...  66.3 us
  transfers between devices with their start and end apart: 9, of which 9 were waited for; matrix products, arithmetic and copies ran while one was open for 6% of the time, Pallas kernels for 0%

commit v1 on v0

v1 whole, which is shorter than its diff:
```python
import functools

import jax
import jax.numpy as jnp
from jax import lax
from jax.sharding import PartitionSpec as P

EPSILON = 1e-06
FLOOR_SCORE = -1e30
SQRT_HALF = 0.7071067811865476
INV_ROOT_TWO_PI = 0.3989422804014327


def layer_norm(values, gain, shift):
    centre = values - jnp.mean(values, axis=-1, keepdims=True)
    inverse = lax.rsqrt(jnp.mean(centre * centre, axis=-1, keepdims=True) + EPSILON)
    scaled = centre * inverse
    return (scaled * gain + shift, scaled, inverse)


def norm_back(grad_normed, scaled, inverse, gain):
    grad_scaled = grad_normed * gain
    first = jnp.mean(grad_scaled, axis=-1, keepdims=True)
    second = jnp.mean(grad_scaled * scaled, axis=-1, keepdims=True)
    return inverse * (grad_scaled - first - scaled * second)


def gelu_parts(inner):
    normal_cdf = 0.5 * (1.0 + lax.erf(inner * SQRT_HALF))
    density = jnp.exp(-0.5 * inner * inner) * INV_ROOT_TWO_PI
    return (inner * normal_cdf, normal_cdf + inner * density)


def head_bias_row(bias, head_size):
    blank = jnp.zeros((bias.shape[0], head_size), jnp.float32)
    joined = jnp.concatenate(
        [bias[:, :head_size].astype(jnp.float32), blank, bias[:, head_size:].astype(jnp.float32)],
        axis=1,
    )
    return joined.reshape(-1)


def gather_weight(block, _):
    count = lax.axis_size("dp")
    rows = block.shape[0] // 8
    own = lax.dynamic_slice_in_dim(block, (lax.axis_index("dp") % 8) * rows, rows, 0)
    if count == 8:
        return lax.all_gather(own, ("tp", "dp"), axis=0, tiled=True)
    return lax.all_gather(block, "tp", axis=0, tiled=True)


def scatter_grad(partial):
    part = lax.psum_scatter(partial, ("tp", "dp"), scatter_dimension=0, tiled=True)
    return lax.all_gather(part, "dp", axis=0, tiled=True).astype(jnp.float32)


def local(
    inputs,
    segment_ids,
    mask_flags,
    mask_token,
    norm_gain,
    norm_shift,
    heads_weight,
    heads_bias,
    proj_weight,
    proj_bias,
    attn_scale,
    mlp_gain,
    mlp_shift,
    up_weight,
    up_bias,
    down_weight,
    down_bias,
    mlp_scale,
    grad_out,
):
    own_rows, slots = mask_flags.shape
    width = inputs.shape[1]
    triple = heads_weight.shape[2]
    head_size = triple // 3
    scale = head_size ** (-0.5)
    own_ids = lax.dynamic_slice_in_dim(segment_ids, lax.axis_index("tp") * own_rows, own_rows, 0)
    valid = (own_ids.reshape(-1, 1) >= 0).astype(jnp.float32)
    flagged = (mask_flags.reshape(-1, 1) == 1).astype(jnp.float32)
    f32, bf16 = jnp.float32, jnp.bfloat16
    dot = functools.partial(lax.dot_general, preferred_element_type=f32)
    nn = (((1,), (0,)), ((), ()))
    nt = (((1,), (1,)), ((), ()))
    tn = (((0,), (0,)), ((), ()))
    heads_all = gather_weight(heads_weight.reshape(width, -1), width // 8)
    proj_all = gather_weight(proj_weight, 0)
    up_all = gather_weight(up_weight, 0)
    down_all = gather_weight(down_weight, 0)
    n_tp = lax.axis_size("tp")
    all_heads_bias = lax.all_gather(heads_bias.astype(f32), "tp", axis=0, tiled=True)
    up_bias_all = lax.all_gather(up_bias.astype(f32), "tp", axis=0, tiled=True)
    heads_now = all_heads_bias.shape[0]
    start_x = valid * (flagged * mask_token.astype(f32) + (1.0 - flagged) * inputs.astype(f32))
    first_gain = norm_gain.astype(f32)
    second_gain = mlp_gain.astype(f32)
    normed1, scaled1, inverse1 = layer_norm(start_x, first_gain, norm_shift.astype(f32))
    normed1 = normed1.astype(bf16)
    heads_cat = jnp.moveaxis(heads_all.reshape(n_tp, width, -1), 0, 1).reshape(width, -1)
    packed = (dot(normed1, heads_cat, nn) + head_bias_row(all_heads_bias, head_size)).astype(bf16)
    blocks = packed.reshape(slots, heads_now, triple)
    query = blocks[..., :head_size]
    keys = blocks[..., head_size:2 * head_size]
    values = blocks[..., 2 * head_size:]
    groups = own_ids[0]
    same = (groups[:, None] == groups[None, :])[None]
    scores = jnp.einsum("qhd,khd->hqk", query, keys, preferred_element_type=f32) * scale
    scores = jnp.where(same, scores, FLOOR_SCORE)
    largest = jnp.max(scores, axis=-1, keepdims=True)
    raised = jnp.exp(scores - largest)
    total = jnp.sum(raised, axis=-1, keepdims=True)
    shares = (raised / total).astype(bf16)
    mixed = jnp.einsum("hqk,khd->qhd", shares, values, preferred_element_type=f32).astype(bf16)
    mixed = mixed.reshape(slots, -1)
    branch1 = dot(mixed, proj_all, nn) + proj_bias.astype(f32)
    middle = start_x + attn_scale.astype(f32) * branch1
    normed2, scaled2, inverse2 = layer_norm(middle, second_gain, mlp_shift.astype(f32))
    normed2 = normed2.astype(bf16)
    up_cat = jnp.moveaxis(up_all.reshape(n_tp, width, -1), 0, 1).reshape(width, -1)
    unit_input = dot(normed2, up_cat, nn) + up_bias_all
    unit_value, derivative = gelu_parts(unit_input)
    unit_low = unit_value.astype(bf16)
    branch2 = dot(unit_low, down_all, nn) + down_bias.astype(f32)
    output = (valid * (middle + mlp_scale.astype(f32) * branch2)).astype(bf16)
    grad_final = valid * grad_out.astype(f32)
    grad_scale2 = jnp.sum(branch2 * grad_final, axis=0)
    grad_branch2 = mlp_scale.astype(f32) * grad_final
    grad_down_bias = jnp.sum(grad_branch2, axis=0)
    grad_low2 = grad_branch2.astype(bf16)
    sum_down = scatter_grad(dot(unit_low, grad_low2, tn).astype(bf16))
    grad_unit = (dot(grad_low2, down_all, nt) * derivative).astype(bf16)
    columns = lambda g: jnp.moveaxis(g.reshape(width, n_tp, -1), 1, 0).reshape(n_tp * width, -1)
    sum_up = scatter_grad(columns(dot(normed2, grad_unit, tn).astype(bf16)))
    grad_up_bias = jnp.sum(grad_unit, axis=0, dtype=f32)
    grad_normed2 = dot(grad_unit, up_cat, nt)
    grad_gain2 = jnp.sum(grad_normed2 * scaled2, axis=0)
    grad_shift2 = jnp.sum(grad_normed2, axis=0)
    grad_middle = grad_final + norm_back(grad_normed2, scaled2, inverse2, second_gain)
    grad_scale1 = jnp.sum(branch1 * grad_middle, axis=0)
    grad_branch1 = attn_scale.astype(f32) * grad_middle
    grad_proj_bias = jnp.sum(grad_branch1, axis=0)
    grad_low1 = grad_branch1.astype(bf16)
    sum_proj = scatter_grad(dot(mixed, grad_low1, tn).astype(bf16))
    grad_mixed = dot(grad_low1, proj_all, nt).astype(bf16).reshape(slots, heads_now, head_size)
    exact = raised / total
    grad_shares = jnp.einsum("qhd,khd->hqk", grad_mixed, values, preferred_element_type=f32)
    centre = jnp.sum(exact * grad_shares, axis=-1, keepdims=True)
    grad_scores = (exact * (grad_shares - centre)).astype(bf16)
    grad_query = jnp.einsum("hqk,khd->qhd", grad_scores, keys, preferred_element_type=f32) * scale
    grad_keys = jnp.einsum("hqk,qhd->khd", grad_scores, query, preferred_element_type=f32) * scale
    grad_values = jnp.einsum("hqk,qhd->khd", shares, grad_mixed, preferred_element_type=f32)
    grad_packed = jnp.concatenate([grad_query, grad_keys, grad_values], axis=-1).astype(bf16)
    grad_packed = grad_packed.reshape(slots, -1)
    sum_heads = scatter_grad(columns(dot(normed1, grad_packed, tn).astype(bf16)))
    sum_heads = sum_heads.reshape(heads_weight.shape)
    bias_sums = jnp.sum(grad_packed, axis=0, dtype=f32).reshape(heads_now, triple)
    grad_normed1 = dot(grad_packed, heads_cat, nt)
    grad_gain1 = jnp.sum(grad_normed1 * scaled1, axis=0)
    grad_shift1 = jnp.sum(grad_normed1, axis=0)
    grad_start = grad_middle + norm_back(grad_normed1, scaled1, inverse1, first_gain)
    grad_inputs = valid * (1.0 - flagged) * grad_start
    grad_token = jnp.sum(valid * flagged * grad_start, axis=0)
    small = jnp.concatenate([
        grad_token, grad_gain1, grad_shift1, grad_proj_bias, grad_scale1, grad_gain2,
        grad_shift2, grad_down_bias, grad_scale2, bias_sums.reshape(-1), grad_up_bias])
    small = lax.psum(small, ("dp", "tp"))
    (sum_token, sum_gain1, sum_shift1, sum_proj_bias, sum_scale1, sum_gain2, sum_shift2,
     sum_down_bias, sum_scale2) = [small[i * width:(i + 1) * width] for i in range(9)]
    me = lax.axis_index("tp")
    bias_sums = small[9 * width:9 * width + heads_now * triple].reshape(heads_now, triple)
    bias_sums = lax.dynamic_slice_in_dim(bias_sums, me * heads_bias.shape[0], heads_bias.shape[0], 0)
    sum_heads_bias = jnp.concatenate([bias_sums[:, :head_size], bias_sums[:, 2 * head_size:]], axis=1)
    sum_up_bias = lax.dynamic_slice_in_dim(
        small[9 * width + heads_now * triple:], me * up_bias.shape[0], up_bias.shape[0], 0)
    return (
        output,
        grad_inputs,
        sum_token,
        sum_gain1,
        sum_shift1,
        sum_heads,
        sum_heads_bias,
        sum_proj,
        sum_proj_bias,
        sum_scale1,
        sum_gain2,
        sum_shift2,
        sum_up,
        sum_up_bias,
        sum_down,
        sum_down_bias,
        sum_scale2,
    )


def solution(mesh):
    placed = (
        P(("dp", "tp"), None),
        P("dp", None),
        P(("dp", "tp"), None),
        P(),
        P(),
        P(),
        P(None, "tp", None),
        P("tp", None),
        P("tp", None),
        P(),
        P(),
        P(),
        P(),
        P(None, "tp"),
        P("tp"),
        P("tp", None),
        P(),
        P(),
        P(("dp", "tp"), None),
    )
    return jax.shard_map(
        local,
        mesh=mesh,
        in_specs=placed,
        out_specs=(
            P(("dp", "tp"), None),
            P(("dp", "tp"), None),
            P(),
            P(),
            P(),
            P(None, "tp", None),
            P("tp", None),
            P("tp", None),
            P(),
            P(),
            P(),
            P(),
            P(None, "tp"),
            P("tp"),
            P("tp", None),
            P(),
            P(),
        ),
        check_vma=False,
    )
```

time: 1100 us -> 804 us (0.73)
  waiting for transfers between devices: 752 us -> 386 us
  matrix products: 143 us -> 186 us
  blocking collectives: 57.1 us -> 87.6 us
    all_gather x4 -> x6, waiting for transfers between devices: 377 us -> 169 us  [the longest x4 134 us: gather_weight(): return lax.all_gather(own, ('tp', 'dp'), axis=0, tiled=True)]
    reduce_scatter x4, waiting for transfers between devices: 308 us -> 217 us  [scatter_grad(): lax.psum_scatter(partial, ('tp', 'dp'), scatter_dimension=0, tiled=True)]
    psum x1 -> x0, waiting for transfers between devices: 66.3 us -> none  [local(): lax.psum((local_grads[0], local_grads[1], local_grads[2], local_grads[3],...]
    all_gather x0 -> x4, blocking collectives: none -> 47.2 us  [the longest x2 20.4 us: scatter_grad(): return lax.all_gather(part, 'dp', axis=0, tiled=True).astype(jnp.float32)]
    dot_general x40 -> x17, matrix products: 143 us -> 166 us  [the longest x1 27.2 us: local(): jnp.einsum('qhd,khd->hqk', grad_mixed, values, preferred_element_type=f32)]
    convert_element_type x18 -> x13, other arithmetic: 16.7 us -> 36.7 us  [the longest x1 30.1 us: local(): grad_scores = (exact * (grad_shares - centre)).astype(bf16)]
    sub x0 -> x1, matrix products: none -> 19.8 us  [local(): raised = jnp.exp(scores - largest)]
    reduce_sum x7 -> x1, other arithmetic: 18.5 us -> 1.06 us  [local(): jnp.sum(grad_packed, axis=0, dtype=f32).reshape(heads_now, triple)]
  transfers between devices with their start and end apart: 9 -> 10, of which waited for: 9 -> 8; matrix products, arithmetic and copies ran while one was open for 6% -> 31% of each run, Pallas kernels for 0% -> 0%
where the time goes in v1:
time: 804 us; the launch traced here: 800 us
  waiting for transfers between devices  386 us (48%)
  matrix products  186 us (23%)
  blocking collectives  87.6 us (11%)
  local copies, waits for them, and re-layouts  68.1 us (8%)
  other arithmetic  55.7 us (7%)
  between operations  15.4 us (2%)
    reduce_scatter x4, waiting for transfers between devices, scatter_grad(): lax.psum_scatter(partial, ('tp', 'dp'), scatter_dimension=0, tiled=True)  217 us
    all_gather x4, waiting for transfers between devices, gather_weight(): return lax.all_gather(own, ('tp', 'dp'), axis=0, tiled=True)  134 us
    psum x1, blocking collectives, local(): small = lax.psum(small, ('dp', 'tp'))  40.5 us
    all_gather x2, waiting for transfers between devices, scatter_grad(): return lax.all_gather(part, 'dp', axis=0, tiled=True).astype(jnp.float32)  35 us
    convert_element_type x1, other arithmetic, local(): grad_scores = (exact * (grad_shares - centre)).astype(bf16)  30.1 us
    dot_general x1, matrix products, local(): jnp.einsum('qhd,khd->hqk', grad_mixed, values, preferred_element_type=f32)  27.2 us
    all_gather x2, blocking collectives, scatter_grad(): return lax.all_gather(part, 'dp', axis=0, tiled=True).astype(jnp.float32)  20.4 us
    sub x1, matrix products, local(): raised = jnp.exp(scores - largest)  19.8 us
  transfers between devices with their start and end apart: 10, of which 8 were waited for; matrix products, arithmetic and copies ran while one was open for 31% of the time, Pallas kernels for 0%

profile of v1, /device:TPU:0, one launch (start us, length us, event | category | flops | bytes accessed | tf_op | source)
XLA Modules:
  0.0 799.6 jit_solution(7235926682024903587)
XLA Ops:
  7.4 1.2 constant_dynamic-slice_fusion.3
  8.6 0.8 copy.81
  9.5 1.4 constant_dynamic-slice_fusion.2
  10.9 0.7 constant_dynamic-slice_fusion.1
  11.7 1.6 constant_dynamic-slice_fusion
  13.4 0.7 compare_reduce_fusion
  14.1 0.7 dynamic-slice_reduce_fusion
  16.8 13.5 %all-gather = f32[4,3,128]{2,1,0:T(4,128)S(1)} all-gather(f32[1,3,128]{2,1,0:T(4,128)S(1)} %bitcast_convert_fusion), channel_id=1, replica_groups=mesh['dp'=8,'tp'=4] {'tp'}, dimensions={0}, use_global_device_ids=true | all-gather | bytes 7680 | tf_op jit(solution)/shard_map/all_gather | solution.py:96
  30.3 0.8 fusion.21
  31.2 0.9 multiply_reduce_fusion.9
  32.4 13.2 %all-gather.1 = f32[4,1,768]{2,1,0:T(1,128)S(1)} all-gather(f32[1,1,768]{2,1,0:T(1,128)S(1)} %reshape.247), channel_id=1, replica_groups=mesh['dp'=8,'tp'=4] {'tp'}, dimensions={0}, use_global_device_ids=true | all-gather | bytes 15360 | tf_op jit(solution)/shard_map/all_gather | solution.py:97
  45.6 30.0 %all-gather.9.cloned.1.call-done = bf16[3072,576]{1,0:T(8,128)(2,1)} async-done(((bf16[96,576]{1,0:T(8,128)(2,1)}), bf16[3072,576]{1,0:T(8,128)(2,1)}) %all-gather.9.cloned.1.call-update) | async-done | bytes 3538960 | tf_op jit(solution)/shard_map/all_gather | solution.py:48
  75.6 8.0 %copy.100 = bf16[4,768,576]{1,0,2:T(4,128)(2,1)} copy(bf16[4,768,576]{2,1,0:T(8,128)(2,1)} %bitcast.70) | data formatting | bytes 7077888 | tf_op jit(solution)/shard_map/reshape | solution.py:104
  83.6 2.5 copy.83
  86.1 1.7 copy-done.11
  87.8 5.3 add_convert_fusion
  93.1 6.3 copy.84
  99.5 19.8 %fusion.53 = (f32[12,832]{1,0:T(8,128)S(1)}, f32[12,832,832]{1,2,0:T(8,128)}) fusion(pred[832,832]{0,1:T(8,128)(4,1)S(1)} %broadcast_compare_fusion, bf16[832,12,192]{0,2,1:T(8,128)(2,1)} %bitcast.56), kind=kOutput, calls=%fused_computation.116 | convolution fusion | flops 1096483584 | bytes 36711424 | tf_op jit(solution)/shard_map/sub | solution.py:115
  119.2 16.0 %fusion.26 = bf16[12,64,832]{2,1,0:T(8,128)(2,1)} fusion(bf16[832,12,192]{0,2,1:T(8,128)(2,1)} %bitcast.57, f32[12,832,832]{1,2,0:T(8,128)} %get-tuple-element.74, f32[12,832]{1,0:T(8,128)S(1)} %get-tuple-element.73), kind=kOutput, calls=%fused_computation.62 | convolution fusion | flops 1080508416 | bytes 38476800 | tf_op jit(solution)/shard_map/hqk,khd->qhd/dot_general | solution.py:118
  135.3 4.9 fusion.50
  140.2 1.4 copy-done.4
  142.1 55.8 %all-gather.13.cloned.1.call-done = bf16[3072,768]{1,0:T(8,128)(2,1)} async-done(((bf16[96,768]{1,0:T(8,128)(2,1)}), bf16[3072,768]{1,0:T(8,128)(2,1)}) %all-gather.13.cloned.1.call-update) | async-done | bytes 4718608 | tf_op jit(solution)/shard_map/all_gather | solution.py:48
  197.9 6.6 copy.86
  204.5 10.7 %multiply_convert_fusion.1 = (bf16[832,3072]{1,0:T(8,128)(2,1)}, f32[832,3072]{1,0:T(8,128)}) fusion(f32[3072]{0:T(1024)S(1)} %bitcast.77, bf16[768,3072]{0,1:T(8,128)(2,1)} %bitcast.64, f32[832,768]{1,0:T(8,128)} %copy-done.4, f32[768]{0:T(1024)S(1)} %convert_element_type.165, f32[768]{0:T(1024)S(1)} %convert_element_type.164, f32[832]{0:T(1024)S(1)} %add_rsqrt_fusion, ...), kind=kOutput, calls=%fused_computation.18 | convolution fusion | flops 3944398848 | bytes 22635008 | tf_op jit(solution)/shard_map/dot_general | solution.py:125
  215.2 48.5 %all-gather.15.cloned.1.call-done = bf16[3072,768]{1,0:T(8,128)(2,1)} async-done(((bf16[96,768]{1,0:T(8,128)(2,1)}), bf16[3072,768]{1,0:T(8,128)(2,1)}) %all-gather.15.cloned.1.call-update) | async-done | bytes 4718608 | tf_op jit(solution)/shard_map/all_gather | solution.py:48
  263.7 11.2 %convert_reduce_fusion = (f32[3072]{0:T(1024)}, bf16[832,3072]{1,0:T(8,128)(2,1)S(1)}) fusion(f32[832,3072]{1,0:T(8,128)} %get-tuple-element.80, f32[3072]{0:T(1024)S(1)} %bitcast.78, bf16[3072,768]{1,0:T(8,128)(2,1)} %all-gather.15.cloned.1.call-done, bf16[832,768]{1,0:T(8,128)(2,1)S(1)} %copy-done.13, f32[768]{0:T(1024)S(1)} %convert_element_type.163, ...), kind=kOutput, calls=%fused_computation.17 | convolution fusion | flops 3961648128 | bytes 21362944 | tf_op jit(solution)/shard_map/dot_general | solution.py:136
  274.9 6.6 multiply_reduce_fusion.2
  281.5 7.7 convolution_convert_fusion.1
  289.1 7.1 convolution_convert_fusion
  296.2 9.7 %reshape.241 = bf16[768,4,768]{2,1,0:T(4,128)(2,1)} reshape(bf16[768,3072]{1,0:T(8,128)(2,1)} %convolution_convert_fusion.1) | data formatting | bytes 9437184 | tf_op jit(solution)/shard_map/reshape | solution.py:137
  306.0 5.1 copy.95
  311.2 4.9 multiply_reduce_fusion.3
  316.1 1.4 copy-done.6
  317.5 2.3 convolution_convert_fusion.3
  319.8 1.8 copy.87
  321.6 27.2 %multiply_reduce_fusion = (f32[12,832]{1,0:T(8,128)S(1)}, f32[12,832,832]{1,2,0:T(8,128)}) fusion(f32[12,832,832]{1,2,0:T(8,128)} %get-tuple-element.74, f32[12,832]{1,0:T(8,128)S(1)} %get-tuple-element.73, bf16[832,12,64]{0,2,1:T(8,128)(2,1)S(1)} %bitcast.74, bf16[832,12,192]{0,2,1:T(8,128)(2,1)} %bitcast.58), kind=kOutput, calls=%fused_computation.2 | convolution fusion | flops 1088166144 | bytes 71743488 | tf_op jit(solution)/shard_map/qhd,khd->hqk/dot_general | solution.py:151
  348.9 30.1 %multiply_convert_fusion = bf16[12,832,832]{1,2,0:T(8,128)(2,1)} fusion(f32[12,832,832]{1,2,0:T(8,128)} %get-tuple-element.78, f32[12,832]{1,0:T(8,128)S(1)} %get-tuple-element.77, f32[12,832,832]{1,2,0:T(8,128)} %get-tuple-element.74, f32[12,832]{1,0:T(8,128)S(1)} %get-tuple-element.73), kind=kLoop, calls=%fused_computation.1 | loop fusion | flops 33226752 | bytes 83146752 | tf_op jit(solution)/shard_map/convert_element_type | solution.py:153
  378.9 3.8 convolution_convert_fusion.4
  382.7 10.4 %multiply_bitcast_fusion = bf16[832,12,64]{0,2,1:T(8,128)(2,1)} fusion(bf16[12,832,832]{1,2,0:T(8,128)(2,1)} %multiply_convert_fusion, bf16[832,12,192]{0,2,1:T(8,128)(2,1)} %bitcast.59), kind=kOutput, calls=%fused_computation.31 | convolution fusion | flops 1064534016 | bytes 20545536 | tf_op jit(solution)/shard_map/hqk,qhd->khd/dot_general | solution.py:155
  393.1 15.3 %fusion.23 = bf16[832,12,64]{0,2,1:T(8,128)(2,1)} fusion(bf16[832,12,64]{0,2,1:T(8,128)(2,1)S(1)} %bitcast.75, f32[12,832,832]{1,2,0:T(8,128)} %get-tuple-element.74, f32[12,832]{1,0:T(8,128)S(1)} %get-tuple-element.73), kind=kOutput, calls=%fused_computation.61 | convolution fusion | flops 1079869440 | bytes 35822592 | tf_op jit(solution)/shard_map/hqk,qhd->khd/dot_general | solution.py:156
  408.5 10.0 %multiply_bitcast_fusion.1 = bf16[832,12,64]{0,2,1:T(8,128)(2,1)S(1)} fusion(bf16[12,832,832]{1,2,0:T(8,128)(2,1)} %multiply_convert_fusion, bf16[832,12,192]{0,2,1:T(8,128)(2,1)} %bitcast.60), kind=kOutput, calls=%fused_computation.32 | convolution fusion | flops 1064534016 | bytes 20545536 | tf_op jit(solution)/shard_map/hqk,khd->qhd/dot_general | solution.py:154
  418.6 1.1 convert_reduce_fusion.1
  419.7 1.9 copy-done.10
  421.7 6.5 convolution_convert_fusion.2
  428.2 5.8 copy.91
  434.0 6.0 copy.103
  440.8 9.7 %fusion.62 = f32[832,768]{1,0:T(8,128)} fusion(bf16[832,3072]{1,0:T(8,128)(2,1)} %get-tuple-element.79, bf16[3072,768]{1,0:T(8,128)(2,1)} %all-gather.15.cloned.1.call-done), kind=kOutput, calls=%fused_computation.117 | convolution fusion | flops 3925868544 | bytes 12386304 | tf_op jit(solution)/shard_map/dot_general | solution.py:128
  450.8 11.5 %multiply_reduce_fusion.4 = (f32[768]{0:T(1024)S(1)}, f32[832]{0:T(1024)S(1)}, f32[832]{0:T(1024)S(1)}, f32[768]{0:T(1024)S(1)}, f32[768]{0:T(1024)S(1)}, /*inde...) fusion(bf16[832,768]{1,0:T(8,128)(2,1)S(1)} %copy-done.3, f32[832]{0:T(1024)S(1)} %copy-done.30, ...), kind=kOutput, calls=%fused_computation.36 | convolution fusion | flops 2960371200 | bytes 18922240 | tf_op jit(solution)/shard_map/dot_general | solution.py:162
  462.4 2.9 multiply_reduce_fusion.5
  465.3 64.1 %reduce-scatter.11.cloned.1.call-done = bf16[96,768]{1,0:T(8,128)(2,1)} async-done(((bf16[3072,768]{1,0:T(8,128)(2,1)}), bf16[96,768]{1,0:T(8,128)(2,1)}) %reduce-scatter.11.cloned.1.call-update) | async-done | bytes 147472 | tf_op jit(solution)/shard_map/reduce_scatter | solution.py:53
  529.6 40.5 %psum.7 = f32[12288]{0:T(1024)S(1)} all-reduce(f32[12288]{0:T(1024)S(1)} %constant_dynamic-update-slice_fusion), channel_id=1, replica_groups=mesh['dp'=8,'tp'=4] {'dp','tp'}, use_global_device_ids=true, to_apply=%region_22.23 | all-reduce | flops 12288 | bytes 98304 | tf_op jit(solution)/shard_map/psum | solution.py:171
  570.2 0.7 dynamic_slice.27
  570.9 0.7 pad_maximum_fusion.1
  572.2 3.4 broadcast_multiply_fusion
  575.6 54.7 %reduce-scatter.7.cloned.1.call-done = bf16[24,768]{1,0:T(8,128)(2,1)} async-done(((bf16[768,768]{1,0:T(8,128)(2,1)}), bf16[24,768]{1,0:T(8,128)(2,1)}) %reduce-scatter.7.cloned.1.call-update) | async-done | bytes 36880 | tf_op jit(solution)/shard_map/reduce_scatter | solution.py:53
  630.4 9.5 %all_gather.37 = bf16[192,768]{1,0:T(8,128)(2,1)S(1)} all-gather(bf16[24,768]{1,0:T(8,128)(2,1)} %reduce-scatter.7.cloned.1.call-done), channel_id=1, replica_groups=mesh['dp'=8,'tp'=4] {'dp'}, dimensions={0}, use_global_device_ids=true | all-gather | bytes 331776 | tf_op jit(solution)/shard_map/all_gather | solution.py:54
  639.9 0.9 convert_element_type.183
  640.8 98.1 %reduce-scatter.13.cloned.1.call-done = bf16[96,576]{1,0:T(8,128)(2,1)} async-done(((bf16[3072,576]{1,0:T(8,128)(2,1)}), bf16[96,576]{1,0:T(8,128)(2,1)}) %reduce-scatter.13.cloned.1.call-update) | async-done | bytes 110608 | tf_op jit(solution)/shard_map/reduce_scatter | solution.py:53
  738.8 10.8 %all_gather.36 = bf16[768,576]{1,0:T(8,128)(2,1)S(1)} all-gather(bf16[96,576]{1,0:T(8,128)(2,1)} %reduce-scatter.13.cloned.1.call-done), channel_id=1, replica_groups=mesh['dp'=8,'tp'=4] {'dp'}, dimensions={0}, use_global_device_ids=true | all-gather | bytes 995328 | tf_op jit(solution)/shard_map/all_gather | solution.py:54
  750.3 1.4 convert.2
  751.7 12.1 %all-gather.17.cloned.1.call-done = bf16[768,768]{1,0:T(8,128)(2,1)} async-done(((bf16[96,768]{1,0:T(8,128)(2,1)}), bf16[768,768]{1,0:T(8,128)(2,1)}) %all-gather.17.cloned.1.call-update) | async-done | bytes 1179664 | tf_op jit(solution)/shard_map/all_gather | solution.py:54
  763.8 2.9 convert_element_type.185
  766.7 22.9 %all-gather.19.cloned.1.call-done = bf16[768,768]{1,0:T(8,128)(2,1)} async-done(((bf16[96,768]{1,0:T(8,128)(2,1)}), bf16[768,768]{1,0:T(8,128)(2,1)}) %all-gather.19.cloned.1.call-update) | async-done | bytes 1179664 | tf_op jit(solution)/shard_map/all_gather | solution.py:54
  789.6 2.8 convert_element_type.187
  (176 shorter events, 5.7 us)
Async XLA Ops:
  7.2 3.7 copy-start
  7.2 9.3 %copy-start.49 = (bf16[3,128]{1,0:T(4,128)(2,1)S(1)}, bf16[3,128]{1,0:T(4,128)(2,1)}, u32[]{:S(2)}) copy-start(bf16[3,128]{1,0:T(4,128)(2,1)} %param.26) | copy-start | bytes 2308
  7.2 9.3 %copy-start.48 = (bf16[768]{0:T(1024)(128)(2,1)S(1)}, bf16[768]{0:T(1024)(128)(2,1)}, u32[]{:S(2)}) copy-start(bf16[768]{0:T(1024)(128)(2,1)} %param.33) | copy-start | bytes 4612
  7.2 9.3 %copy-start.39 = (bf16[768]{0:T(1024)(128)(2,1)S(1)}, bf16[768]{0:T(1024)(128)(2,1)}, u32[]{:S(2)}) copy-start(bf16[768]{0:T(1024)(128)(2,1)} %param.22) | copy-start | bytes 4612
  7.2 9.3 %copy-start.40 = (bf16[768]{0:T(1024)(128)(2,1)S(1)}, bf16[768]{0:T(1024)(128)(2,1)}, u32[]{:S(2)}) copy-start(bf16[768]{0:T(1024)(128)(2,1)} %param.23) | copy-start | bytes 4612
  7.3 9.4 %copy-start.41 = (bf16[768]{0:T(1024)(128)(2,1)S(1)}, bf16[768]{0:T(1024)(128)(2,1)}, u32[]{:S(2)}) copy-start(bf16[768]{0:T(1024)(128)(2,1)} %param.29) | copy-start | bytes 4612
  7.3 9.4 %copy-start.42 = (bf16[768]{0:T(1024)(128)(2,1)S(1)}, bf16[768]{0:T(1024)(128)(2,1)}, u32[]{:S(2)}) copy-start(bf16[768]{0:T(1024)(128)(2,1)} %param.30) | copy-start | bytes 4612
  7.3 9.4 %copy-start.43 = (bf16[768]{0:T(1024)(128)(2,1)S(1)}, bf16[768]{0:T(1024)(128)(2,1)}, u32[]{:S(2)}) copy-start(bf16[768]{0:T(1024)(128)(2,1)} %param.36) | copy-start | bytes 4612
  7.3 9.4 %copy-start.44 = (bf16[768]{0:T(1024)(128)(2,1)S(1)}, bf16[768]{0:T(1024)(128)(2,1)}, u32[]{:S(2)}) copy-start(bf16[768]{0:T(1024)(128)(2,1)} %param.24) | copy-start | bytes 4612
  7.3 9.4 %copy-start.45 = (bf16[768]{0:T(1024)(128)(2,1)S(1)}, bf16[768]{0:T(1024)(128)(2,1)}, u32[]{:S(2)}) copy-start(bf16[768]{0:T(1024)(128)(2,1)} %param.28) | copy-start | bytes 4612
  7.3 9.5 %copy-start.46 = (bf16[768]{0:T(1024)(128)(2,1)S(1)}, bf16[768]{0:T(1024)(128)(2,1)}, u32[]{:S(2)}) copy-start(bf16[768]{0:T(1024)(128)(2,1)} %param.31) | copy-start | bytes 4612
  7.3 23.0 %copy-start.2 = (bf16[832,768]{1,0:T(8,128)(2,1)S(1)}, bf16[832,768]{1,0:T(8,128)(2,1)}, u32[]{:S(2)}) copy-start(bf16[832,768]{1,0:T(8,128)(2,1)} %param.19) | copy-start | bytes 3833860
  7.3 68.2 %all-gather.9.cloned.1.call-start = ((), (), s32[]{:S(2)}) async-start(), calls=%async_computation.4 | async-start | bytes 4055040 | tf_op jit(solution)/shard_map/all_gather | solution.py:48
  9.4 125.8 %all-gather.11.cloned.1.call-start = ((), (), s32[]{:S(2)}) async-start(), calls=%async_computation.5 | async-start | bytes 1216512 | tf_op jit(solution)/shard_map/all_gather | solution.py:48
  10.9 187.0 %all-gather.13.cloned.1.call-start = ((), (), s32[]{:S(2)}) async-start(), calls=%async_computation.6 | async-start | bytes 4866048 | tf_op jit(solution)/shard_map/all_gather | solution.py:48
  11.7 252.0 %all-gather.15.cloned.1.call-start = ((), (), s32[]{:S(2)}) async-start(), calls=%async_computation.7 | async-start | bytes 4866048 | tf_op jit(solution)/shard_map/all_gather | solution.py:48
  13.3 437.2 %reduce-scatter.9.cloned.1.call-start = ((), (), s32[]{:S(2)}) async-start(), calls=%async_computation.9 | async-start | bytes 4866048 | tf_op jit(solution)/shard_map/reduce_scatter | solution.py:53
  14.1 121.2 %copy-start.16 = (f32[832]{0:T(1024)}, f32[832]{0:T(1024)S(1)}, u32[]{:S(2)}) copy-start(f32[832]{0:T(1024)S(1)} %convert_element_type.150) | copy-start | bytes 9988
  15.4 295.7 %copy-start.14 = (f32[832]{0:T(1024)}, f32[832]{0:T(1024)S(1)}, u32[]{:S(2)}) copy-start(f32[832]{0:T(1024)S(1)} %convert_element_type.149) | copy-start | bytes 9988
  16.0 119.2 %copy-start.18 = (f32[832]{0:T(1024)}, f32[832]{0:T(1024)S(1)}, u32[]{:S(2)}) copy-start(f32[832]{0:T(1024)S(1)} %get-tuple-element.72) | copy-start | bytes 9988
  16.6 118.7 %copy-start.20 = (f32[768]{0:T(1024)}, f32[768]{0:T(1024)S(1)}, u32[]{:S(2)}) copy-start(f32[768]{0:T(1024)S(1)} %convert_element_type.151) | copy-start | bytes 9220
  16.6 69.4 %copy-start.27 = (f32[768]{0:T(1024)}, f32[768]{0:T(1024)S(1)}, u32[]{:S(2)}) copy-start(f32[768]{0:T(1024)S(1)} %convert_element_type.154) | copy-start | bytes 9220
  16.7 272.4 %copy-start.33 = (f32[768]{0:T(1024)}, f32[768]{0:T(1024)S(1)}, u32[]{:S(2)}) copy-start(f32[768]{0:T(1024)S(1)} %convert_element_type.163) | copy-start | bytes 9220
  16.7 69.3 %copy-start.35 = (f32[768]{0:T(1024)}, f32[768]{0:T(1024)S(1)}, u32[]{:S(2)}) copy-start(f32[768]{0:T(1024)S(1)} %convert_element_type.155) | copy-start | bytes 9220
  31.1 54.9 %copy-start.22 = (f32[832]{0:T(1024)}, f32[832]{0:T(1024)S(1)}, u32[]{:S(2)}) copy-start(f32[832]{0:T(1024)S(1)} %broadcast_multiply_fusion.6) | copy-start | bytes 9988
  32.1 54.0 %copy-start.29 = (f32[832]{0:T(1024)}, f32[832]{0:T(1024)S(1)}, u32[]{:S(2)}) copy-start(f32[832]{0:T(1024)S(1)} %add_rsqrt_fusion.1) | copy-start | bytes 9988
  86.1 1.8 copy-start.11
  140.2 1.4 copy-start.4
  204.5 59.2 %copy-start.13 = (bf16[832,768]{1,0:T(8,128)(2,1)S(1)}, bf16[832,768]{1,0:T(8,128)(2,1)}, u32[]{:S(2)}) copy-start(bf16[832,768]{1,0:T(8,128)(2,1)} %param.37) | copy-start | bytes 3833860
  204.5 70.3 %slice-start = ((s8[4718592]{0:T(1024)(128)(4,1)}), s8[524288]{0:T(1024)(128)(4,1)S(1)}, s32[]{:S(2)}) async-start(s8[4718592]{0:T(1024)(128)(4,1)} %bitcast.65), calls=%async_computation.14 | async-start | bytes 1048576
  263.7 11.2 %copy-start.5 = (f32[832,768]{1,0:T(8,128)S(1)}, f32[832,768]{1,0:T(8,128)}, u32[]{:S(2)}) copy-start(f32[832,768]{1,0:T(8,128)} %copy-done.4) | copy-start | bytes 7667716
  263.7 11.2 %slice-start.1 = ((s8[4718592]{0:T(1024)(128)(4,1)}), s8[4194304]{0:T(1024)(128)(4,1)S(1)}, s32[]{:S(2)}) async-start(s8[4718592]{0:T(1024)(128)(4,1)} %bitcast.65), calls=%async_computation.15 | async-start | bytes 8388608
  281.5 7.7 copy-start.51
  311.1 218.3 %reduce-scatter.11.cloned.1.call-start = ((), (), s32[]{:S(2)}) async-start(), calls=%async_computation.11 | async-start | bytes 4866048 | tf_op jit(solution)/shard_map/reduce_scatter | solution.py:53
  311.2 6.4 copy-start.50
  316.1 1.4 copy-start.6
  348.8 281.6 %reduce-scatter.7.cloned.1.call-start = ((), (), s32[]{:S(2)}) async-start(), calls=%async_computation.8 | async-start | bytes 1216512 | tf_op jit(solution)/shard_map/reduce_scatter | solution.py:53
  348.9 30.1 %copy-start.7 = (f32[832,768]{1,0:T(8,128)S(1)}, f32[832,768]{1,0:T(8,128)}, u32[]{:S(2)}) copy-start(f32[832,768]{1,0:T(8,128)} %copy-done.6) | copy-start | bytes 7667716
  408.5 330.4 %reduce-scatter.13.cloned.1.call-start = ((), (), s32[]{:S(2)}) async-start(), calls=%async_computation.13 | async-start | bytes 4055040 | tf_op jit(solution)/shard_map/reduce_scatter | solution.py:53
  408.5 10.0 %copy-start.9 = (bf16[832,12,64]{0,2,1:T(8,128)(2,1)S(1)}, bf16[832,12,64]{0,2,1:T(8,128)(2,1)}, u32[]{:S(2)}) copy-start(bf16[832,12,64]{0,2,1:T(8,128)(2,1)} %multiply_bitcast_fusion) | copy-start | bytes 3833860
  408.5 10.0 %copy-start.12 = (bf16[832,12,64]{0,2,1:T(8,128)(2,1)S(1)}, bf16[832,12,64]{0,2,1:T(8,128)(2,1)}, u32[]{:S(2)}) copy-start(bf16[832,12,64]{0,2,1:T(8,128)(2,1)} %fusion.23) | copy-start | bytes 3833860
  418.5 3.1 copy-start.3
  418.5 3.1 copy-start.15
  418.6 3.1 copy-start.17
  418.6 3.1 copy-start.19
  418.6 3.1 copy-start.21
  418.6 3.1 copy-start.23
  418.6 3.1 copy-start.28
  418.6 3.1 copy-start.30
  418.6 3.1 copy-start.36
  419.7 1.9 copy-start.10
  440.0 0.7 copy-start.47
  440.0 323.8 %all-gather.17.cloned.1.call-start = ((), (), s32[]{:S(2)}) async-start(), calls=%async_computation.10 | async-start | bytes 1327104 | tf_op jit(solution)/shard_map/all_gather | solution.py:54
  440.8 10.0 %copy-start.34 = (f32[768]{0:T(1024)S(1)}, f32[768]{0:T(1024)}, u32[]{:S(2)}) copy-start(f32[768]{0:T(1024)} %copy-done.33) | copy-start | bytes 9220
  450.5 11.8 %copy-start.26 = (f32[832]{0:T(1024)S(1)}, f32[832]{0:T(1024)}, u32[]{:S(2)}) copy-start(f32[832]{0:T(1024)} %get-tuple-element.53) | copy-start | bytes 9988
  450.5 339.1 %all-gather.19.cloned.1.call-start = ((), (), s32[]{:S(2)}) async-start(), calls=%async_computation.12 | async-start | bytes 1327104 | tf_op jit(solution)/shard_map/all_gather | solution.py:54
  450.8 11.5 %copy-start.8 = (f32[832,768]{1,0:T(8,128)S(1)}, f32[832,768]{1,0:T(8,128)}, u32[]{:S(2)}) copy-start(f32[832,768]{1,0:T(8,128)} %copy-done.6) | copy-start | bytes 7667716
  462.3 67.1 %copy-start.25 = (f32[768]{0:T(1024)S(1)}, f32[768]{0:T(1024)}, u32[]{:S(2)}) copy-start(f32[768]{0:T(1024)} %get-tuple-element.42) | copy-start | bytes 9220
  462.3 67.1 %copy-start.24 = (f32[768]{0:T(1024)S(1)}, f32[768]{0:T(1024)}, u32[]{:S(2)}) copy-start(f32[768]{0:T(1024)} %get-tuple-element.41) | copy-start | bytes 9220
  462.3 67.1 %copy-start.38 = (f32[768]{0:T(1024)S(1)}, f32[768]{0:T(1024)}, u32[]{:S(2)}) copy-start(f32[768]{0:T(1024)} %get-tuple-element.34) | copy-start | bytes 9220
  462.3 67.2 %copy-start.37 = (f32[768]{0:T(1024)S(1)}, f32[768]{0:T(1024)}, u32[]{:S(2)}) copy-start(f32[768]{0:T(1024)} %get-tuple-element.40) | copy-start | bytes 9220
  462.4 67.2 %copy-start.32 = (f32[3072]{0:T(1024)S(1)}, f32[3072]{0:T(1024)}, u32[]{:S(2)}) copy-start(f32[3072]{0:T(1024)} %get-tuple-element.82) | copy-start | bytes 36868
  462.4 109.8 %copy-start.31 = (f32[832]{0:T(1024)S(1)}, f32[832]{0:T(1024)}, u32[]{:S(2)}) copy-start(f32[832]{0:T(1024)} %get-tuple-element.71) | copy-start | bytes 9988
  763.8 28.7 %copy-start.1 = (bf16[768,768]{1,0:T(8,128)(2,1)S(1)}, bf16[768,768]{1,0:T(8,128)(2,1)}, u32[]{:S(2)}) copy-start(bf16[768,768]{1,0:T(8,128)(2,1)} %param.32) | copy-start | bytes 3538948
Sparse Core Ops, SparseCore 0:
  11.6 63.8 all-gather.8
  79.0 52.6 all-gather.10
  135.2 62.5 all-gather.12
  201.2 62.4 all-gather.14
  311.2 105.7 reduce-scatter.8
  423.3 106.0 reduce-scatter.10
  535.0 95.2 reduce-scatter.6
  635.8 103.0 reduce-scatter.12
  740.7 23.0 all-gather.16
  765.5 24.0 all-gather.18
